TPU v7x, 32 devices: a whole 2x2x4 slice. The times are simulated.
32 devices in a mesh: seq: 4 (over y, x), img: 2 (over core), dp: 4 (over z).
Axes of the slice: x: 2, y: 2, z: 4, core: 2. Of those that a mesh axis runs over, the one named last changes fastest.
Arguments:
- queries: bfloat16 [512, 8192], P('seq', 'dp'), may hold values from -22 to 22
- out_grad: bfloat16 [512, 8192], P('seq', 'dp'), may hold values from -600 to 600
- token_image: int32 [512], P('seq'), may hold values from -1 to 1, as said below
- unnormed_keys: bfloat16 [2, 6432, 1024], P('img', 'seq', 'dp'), may hold values from -14 to 14
- values: bfloat16 [2, 6432, 1024], P('img', 'seq', 'dp'), may hold values from -6 to 6
- key_gain: float32 [128], replicated, may hold values from 0.1 to 1.9
- tile_count: int32 [2], replicated, may hold values from 1 to 4, as said below
- key_projection_matrix: bfloat16 [8192, 1024], P('dp', 'seq'), may hold values from -0.1875 to 0.1875
- value_projection_matrix: bfloat16 [8192, 1024], P('dp', 'seq'), may hold values from -0.1875 to 0.1875
Outputs:
- feature_grad: bfloat16 [2, 6432, 8192], P('img', 'seq', 'dp')
Inputs may be any that keep to these rules, and one draw needn't show every extreme that they name: `token_image`: in each block of 128 tokens (one index of seq) at most 16 tokens name one image, and some image is named by exactly 16; -1 marks a token that attends no image. `tile_count`: some image has 4 tiles.
All inputs are finite; a program needn't handle non-finite values.
Results may differ from a plain program's by a relative error of at most 0.0067.
Values may be sent and summed in bfloat16 or wider, within the bound.
A program may use at most 128 MiB of HBM per device.

v0:
```python
import jax
import jax.numpy as jnp
from jax import lax
from jax.sharding import PartitionSpec as P

QUERY_HEAD_COUNT = 64
KEY_VALUE_HEADS = 8
HEAD_WIDTH = 128
TILE_TOK = 1601
TILE_ROWS = 1608
CAP = 16


epsilon = 1e-05
masked = -1e30


def body(
    queries,
    out_grad,
    token_image,
    unnormed_keys,
    values,
    key_gain,
    tile_count,
    key_projection_matrix,
    value_projection_matrix,
):
    image_number = lax.axis_index("img")
    seq_index = lax.axis_index("seq")
    attends = token_image == image_number
    slot_rank = jnp.cumsum(attends.astype(jnp.int32)) - 1
    picker = (
        attends[None, :] & (slot_rank[None, :] == jnp.arange(CAP, dtype=jnp.int32)[:, None])
    ).astype(jnp.bfloat16)
    packed_query = jnp.dot(picker, queries, preferred_element_type=jnp.float32).astype(jnp.bfloat16)
    packed_grad = jnp.dot(picker, out_grad, preferred_element_type=jnp.float32).astype(jnp.bfloat16)
    text_query, text_grad = (
        lax.all_gather(packed_query, "seq", axis=0, tiled=True),
        lax.all_gather(packed_grad, "seq", axis=0, tiled=True),
    )
    key_rows = unnormed_keys.shape[1]
    key_width = unnormed_keys.shape[2]
    key_heads = key_width // HEAD_WIDTH
    group_length = QUERY_HEAD_COUNT // KEY_VALUE_HEADS
    text_rows = text_query.shape[0]
    score_scale = HEAD_WIDTH ** (-0.5)
    unnormed_float = unnormed_keys[0].astype(jnp.float32).reshape(key_rows, key_heads, HEAD_WIDTH)
    inverse = lax.rsqrt(jnp.mean(unnormed_float * unnormed_float, axis=-1, keepdims=True) + epsilon)
    unit_key = unnormed_float * inverse
    normed = (unit_key * key_gain).astype(jnp.bfloat16)
    value_heads = values[0].reshape(key_rows, key_heads, HEAD_WIDTH)
    query_heads = text_query.reshape(text_rows, key_heads, group_length, HEAD_WIDTH)
    grad_heads = text_grad.reshape(text_rows, key_heads, group_length, HEAD_WIDTH)
    row_global = seq_index * key_rows + jnp.arange(key_rows, dtype=jnp.int32)
    tile_limit = jnp.sum(
        jnp.where(jnp.arange(tile_count.shape[0], dtype=jnp.int32) == image_number, tile_count, 0)
    )
    live_rows = (row_global // TILE_ROWS < tile_limit) & (row_global % TILE_ROWS < TILE_TOK)
    scores = (
        jnp.einsum("rhge,khe->hgrk", query_heads, normed, preferred_element_type=jnp.float32)
        * score_scale
    )
    scores = jnp.where(live_rows, scores, masked)
    grad_probs = jnp.einsum(
        "rhge,khe->hgrk", grad_heads, value_heads, preferred_element_type=jnp.float32
    )
    row_top = lax.pmax(jnp.max(scores, axis=-1), "seq")
    exponent = jnp.exp(scores - row_top[..., None])
    row_total = lax.psum(jnp.sum(exponent, axis=-1), "seq")
    probabilities = exponent / row_total[..., None]
    inner_sum = lax.psum(jnp.sum(probabilities * grad_probs, axis=-1), "seq")
    probs_low = probabilities.astype(jnp.bfloat16)
    score_grad = (probabilities * (grad_probs - inner_sum[..., None])).astype(jnp.bfloat16)
    value_gradient = jnp.einsum(
        "hgrk,rhge->khe", probs_low, grad_heads, preferred_element_type=jnp.float32
    )
    normalized_gradient = (
        jnp.einsum("hgrk,rhge->khe", score_grad, query_heads, preferred_element_type=jnp.float32)
        * score_scale
    )
    unit_grad = normalized_gradient * key_gain
    key_gradient = inverse * (
        unit_grad - unit_key * jnp.mean(unit_grad * unit_key, axis=-1, keepdims=True)
    )
    key_reduced_precision = key_gradient.astype(jnp.bfloat16).reshape(key_rows, key_width)
    value_reduced_precision = value_gradient.astype(jnp.bfloat16).reshape(key_rows, key_width)
    key_all, value_all = (
        lax.all_gather(key_reduced_precision, "dp", axis=1, tiled=True),
        lax.all_gather(value_reduced_precision, "dp", axis=1, tiled=True),
    )
    contracting = (((1,), (1,)), ((), ()))
    partial_value = lax.dot_general(
        key_all,
        lax.all_gather(key_projection_matrix, "seq", axis=1, tiled=True),
        contracting,
        preferred_element_type=jnp.float32,
    )
    feature_sum = partial_value + lax.dot_general(
        value_all,
        lax.all_gather(value_projection_matrix, "seq", axis=1, tiled=True),
        contracting,
        preferred_element_type=jnp.float32,
    )
    return feature_sum.astype(jnp.bfloat16)[None]


def solution(mesh):
    in_specs = (
        P("seq", "dp"),
        P("seq", "dp"),
        P("seq"),
        P("img", "seq", "dp"),
        P("img", "seq", "dp"),
        P(),
        P(),
        P("dp", "seq"),
        P("dp", "seq"),
    )
    out_specs = P("img", "seq", "dp")
    return jax.shard_map(body, mesh=mesh, in_specs=in_specs, out_specs=out_specs, check_vma=False)
```

profile of v0, /device:TPU:0, one launch (start us, length us, event | category | flops | bytes accessed | tf_op | source)
XLA Modules:
  0.0 352.9 jit_solution(12412699333056332310)
XLA Ops:
  6.5 0.0 copy-start
  6.5 0.0 all-gather.5.cloned.1.call-start
  6.5 0.0 copy-start.8
  6.6 2.4 copy.17
  9.0 1.7 copy.19
  10.8 1.6 multiply_reduce_fusion
  12.4 0.0 copy-done.9
  12.4 0.0 copy-start.6
  12.4 0.1 copy.18
  12.5 0.2 reduce-window.8
  12.7 0.1 add_reduce_fusion
  12.8 0.2 convolution_convert_fusion.1
  13.0 10.5 %all_gather.18 = bf16[64,2048]{1,0:T(8,128)(2,1)S(1)} all-gather(bf16[16,2048]{1,0:T(8,128)(2,1)S(1)} %convolution_convert_fusion.1), channel_id=1, replica_groups=mesh['seq'=4,'img'=2,'dp'=4] {'seq'}, dimensions={0}, use_global_device_ids=true | all-gather | bytes 327680 | tf_op jit(solution)/shard_map/all_gather | solution.py:39
  23.5 0.0 copy-done.11
  23.5 0.6 fusion.53
  24.2 0.0 copy-done.8
  24.2 0.5 broadcast_multiply_fusion.1
  24.7 0.7 fusion.43
  25.4 3.6 %bitcast_reduce_fusion = (f32[2,8,64]{2,1,0:T(8,128)S(1)}, f32[2,1608,64,8]{1,2,3,0:T(8,128)}) fusion(pred[1608]{0:T(1024)(128)(4,1)S(1)} %fusion.43, bf16[64,2,8,128]{3,2,1,0:T(8,128)(2,1)S(1)} %bitcast.71, f32[1608,2,128]{2,0,1:T(8,128)S(1)} %copy.19, f32[128]{0:T(128)S(1)} %copy-done.8, f32[1608,2]{0,1:T(2,128)S(1)} %add_rsqrt_fusion), kind=kOutput, calls=%fused_computation.7 | convolution fusion | flops 427701248 | bytes 8514184 | tf_op jit(solution)/shard_map/rhge,khe->hgrk/dot_general | solution.py:61
  29.0 9.2 %pmax.7 = f32[2,8,64]{2,1,0:T(8,128)S(1)} all-reduce(f32[2,8,64]{2,1,0:T(8,128)S(1)} %get-tuple-element.9), channel_id=1, replica_groups=mesh['seq'=4,'img'=2,'dp'=4] {'seq'}, use_global_device_ids=true, to_apply=%region_4.5 | all-reduce | flops 1024 | bytes 8192 | tf_op jit(solution)/shard_map/pmax | solution.py:68
  38.3 4.4 %fusion.6 = f32[2,8,64]{2,1,0:T(8,128)S(1)} fusion(f32[2,1608,64,8]{1,2,3,0:T(8,128)} %get-tuple-element.10, f32[2,8,64]{2,1,0:T(8,128)S(1)} %pmax.7, pred[1608]{0:T(1024)(128)(4,1)S(1)} %fusion.43), kind=kLoop, calls=%fused_computation.12 | loop fusion | flops 6585344 | bytes 6596168 | tf_op jit(solution)/shard_map/reduce_sum | solution.py:70
  42.7 9.1 %psum.14 = f32[2,8,64]{2,1,0:T(8,128)S(1)} all-reduce(f32[2,8,64]{2,1,0:T(8,128)S(1)} %fusion.6), channel_id=1, replica_groups=mesh['seq'=4,'img'=2,'dp'=4] {'seq'}, use_global_device_ids=true, to_apply=%region_6.7 | all-reduce | flops 1024 | bytes 8192 | tf_op jit(solution)/shard_map/psum | solution.py:70
  51.8 0.2 convolution_convert_fusion
  52.0 8.0 %all_gather.19 = bf16[64,2048]{1,0:T(8,128)(2,1)S(1)} all-gather(bf16[16,2048]{1,0:T(8,128)(2,1)S(1)} %convolution_convert_fusion), channel_id=1, replica_groups=mesh['seq'=4,'img'=2,'dp'=4] {'seq'}, dimensions={0}, use_global_device_ids=true | all-gather | bytes 327680 | tf_op jit(solution)/shard_map/all_gather | solution.py:40
  60.0 0.0 copy-done.2
  60.0 1.1 reshape_squeeze.3
  61.1 6.4 %fusion = (f32[2,8,64]{2,1,0:T(8,128)S(1)}, f32[2,64,8,1608]{3,1,2,0:T(8,128)}) fusion(f32[2,8,64]{2,1,0:T(8,128)S(1)} %psum.14, f32[2,8,64]{2,1,0:T(8,128)S(1)} %pmax.7, f32[2,1608,64,8]{1,2,3,0:T(8,128)} %get-tuple-element.10, pred[1608]{0:T(1024)(128)(4,1)S(1)} %fusion.43, bf16[1608,2,128,1]{2,1,0,3:T(2,128)(2,1)} %bitcast.77, ...), kind=kOutput, calls=%fused_computation.3 | convolution fusion | flops 431406080 | bytes 14272072 | tf_op jit(solution)/shard_map/rhge,khe->hgrk/dot_general | solution.py:65
  67.5 9.1 %psum.15 = f32[2,8,64]{2,1,0:T(8,128)S(1)} all-reduce(f32[2,8,64]{2,1,0:T(8,128)S(1)} %get-tuple-element.11), channel_id=1, replica_groups=mesh['seq'=4,'img'=2,'dp'=4] {'seq'}, use_global_device_ids=true, to_apply=%region_8.9 | all-reduce | flops 1024 | bytes 8192 | tf_op jit(solution)/shard_map/psum | solution.py:72
  76.6 0.0 copy-start.10
  76.6 7.2 %fusion.54 = (bf16[2,8,64,1608]{3,2,1,0:T(8,128)(2,1)}, bf16[2,8,64,1608]{3,2,1,0:T(8,128)(2,1)S(1)}) fusion(f32[2,8,64]{2,1,0:T(8,128)S(1)} %psum.14, f32[2,8,64]{2,1,0:T(8,128)S(1)} %pmax.7, f32[2,1608,64,8]{1,2,3,0:T(8,128)} %get-tuple-element.10, pred[1608]{0:T(1024)(128)(4,1)S(1)} %fusion.43, f32[2,8,64]{2,1,0:T(8,128)S(1)} %psum.15, ...), kind=kLoop, calls=%fused_computation.63 | loop fusion | flops 13172736 | bytes 19773000 | tf_op jit(solution)/shard_map/convert_element_type | solution.py:73
  83.9 2.9 multiply_reduce_fusion.1
  86.8 1.0 multiply_convert_fusion
  87.8 1.3 copy.25
  89.1 0.0 all-gather.5.cloned.1.call-update
  89.1 0.0 all-gather.7.cloned.1.call-start
  89.2 0.7 all-gather.7.cloned.1.call-update
  89.9 0.2 all-gather.9.cloned.1.call-start
  90.1 4.4 %fusion.26 = bf16[1608,2,128]{2,0,1:T(8,128)(2,1)S(1)} fusion(bf16[64,2,8,128]{3,2,1,0:T(8,128)(2,1)S(1)} %bitcast.79, bf16[2,8,64,1608]{3,2,1,0:T(8,128)(2,1)} %get-tuple-element.7), kind=kOutput, calls=%fused_computation.22 | convolution fusion | flops 421939200 | bytes 4378624 | tf_op jit(solution)/shard_map/hgrk,rhge->khe/dot_general | solution.py:75
  94.5 1.3 copy.27
  95.7 0.0 all-gather.9.cloned.1.call-update
  95.8 0.0 all-gather.11.cloned.1.call-start
  95.8 0.5 all-gather.11.cloned.1.call-update
  96.3 61.0 %all-gather.5.cloned.1.call-done = bf16[1608,1024]{0,1:T(8,128)(2,1)} async-done(((bf16[1608,256]{0,1:T(8,128)(2,1)}), bf16[1608,1024]{0,1:T(8,128)(2,1)}) %all-gather.5.cloned.1.call-update) | async-done | bytes 3293200 | tf_op jit(solution)/shard_map/all_gather | solution.py:89
  157.3 52.9 %all-gather.7.cloned.1.call-done = bf16[2048,1024]{1,0:T(8,128)(2,1)} async-done(((bf16[2048,256]{1,0:T(8,128)(2,1)}), bf16[2048,1024]{1,0:T(8,128)(2,1)}) %all-gather.7.cloned.1.call-update) | async-done | bytes 4194320 | tf_op jit(solution)/shard_map/all_gather | solution.py:95
  210.2 13.1 %fusion.55 = f32[1608,2048]{1,0:T(8,128)} fusion(bf16[1608,1024]{0,1:T(8,128)(2,1)} %all-gather.5.cloned.1.call-done, bf16[2048,1024]{1,0:T(8,128)(2,1)} %all-gather.7.cloned.1.call-done), kind=kOutput, calls=%fused_computation.64 | convolution fusion | flops 6744440832 | bytes 20660224 | tf_op jit(solution)/shard_map/dot_general | solution.py:93
  223.3 56.2 %all-gather.9.cloned.1.call-done = bf16[1608,1024]{0,1:T(8,128)(2,1)} async-done(((bf16[1608,256]{0,1:T(8,128)(2,1)}), bf16[1608,1024]{0,1:T(8,128)(2,1)}) %all-gather.9.cloned.1.call-update) | async-done | bytes 3293200 | tf_op jit(solution)/shard_map/all_gather | solution.py:90
  279.6 52.8 %all-gather.11.cloned.1.call-done = bf16[2048,1024]{1,0:T(8,128)(2,1)} async-done(((bf16[2048,256]{1,0:T(8,128)(2,1)}), bf16[2048,1024]{1,0:T(8,128)(2,1)}) %all-gather.11.cloned.1.call-update) | async-done | bytes 4194320 | tf_op jit(solution)/shard_map/all_gather | solution.py:101
  332.3 14.0 %fusion.4 = bf16[1,1608,2048]{2,1,0:T(8,128)(2,1)} fusion(f32[1608,2048]{1,0:T(8,128)} %fusion.55, bf16[1608,1024]{0,1:T(8,128)(2,1)} %all-gather.9.cloned.1.call-done, bf16[2048,1024]{1,0:T(8,128)(2,1)} %all-gather.11.cloned.1.call-done), kind=kOutput, calls=%fused_computation.10 | convolution fusion | flops 6751027200 | bytes 27246592 | tf_op jit(solution)/shard_map/dot_general | solution.py:99
  (21 shorter events, 0.1 us)
Async XLA Ops:
  6.5 6.3 %copy-start = (bf16[128,2048]{1,0:T(8,128)(2,1)S(1)}, bf16[128,2048]{1,0:T(8,128)(2,1)}, u32[]{:S(2)}) copy-start(bf16[128,2048]{1,0:T(8,128)(2,1)} %param.9) | copy-start | bytes 1572868
  6.5 5.8 %copy-start.9 = (s32[128]{0:T(128)S(1)}, s32[128]{0:T(128)}, u32[]{:S(2)}) copy-start(s32[128]{0:T(128)} %param.11) | copy-start | bytes 1540
  6.5 150.8 %all-gather.5.cloned.1.call-start = ((), (), s32[]{:S(2)}) async-start(), calls=%async_computation | async-start | bytes 4259840 | tf_op jit(solution)/shard_map/all_gather | solution.py:89
  6.5 17.0 %copy-start.11 = (s32[2]{0:T(128)S(1)}, s32[2]{0:T(128)}, u32[]{:S(2)}) copy-start(s32[2]{0:T(128)} %param.15) | copy-start | bytes 28
  6.5 17.6 %copy-start.8 = (f32[128]{0:T(128)S(1)}, f32[128]{0:T(128)}, u32[]{:S(2)}) copy-start(f32[128]{0:T(128)} %param.14) | copy-start | bytes 1540
  12.4 13.0 %copy-start.6 = (pred[128]{0:T(512)(128)(4,1)}, pred[128]{0:T(512)(128)(4,1)S(1)}, u32[]{:S(2)}) copy-start(pred[128]{0:T(512)(128)(4,1)S(1)} %get-tuple-element.6) | copy-start | bytes 388
  12.8 12.6 %copy-start.4 = (s32[128]{0:T(128)}, s32[128]{0:T(128)S(1)}, u32[]{:S(2)}) copy-start(s32[128]{0:T(128)S(1)} %add_reduce_fusion) | copy-start | bytes 1540
  29.0 22.8 %copy-start.3 = (bf16[128,2048]{1,0:T(8,128)(2,1)S(1)}, bf16[128,2048]{1,0:T(8,128)(2,1)}, u32[]{:S(2)}) copy-start(bf16[128,2048]{1,0:T(8,128)(2,1)} %param.10) | copy-start | bytes 1572868
  29.0 22.8 %copy-start.5 = (s32[128]{0:T(128)S(1)}, s32[128]{0:T(128)}, u32[]{:S(2)}) copy-start(s32[128]{0:T(128)} %copy-done.4) | copy-start | bytes 1540
  29.0 22.8 %copy-start.7 = (pred[128]{0:T(512)(128)(4,1)S(1)}, pred[128]{0:T(512)(128)(4,1)}, u32[]{:S(2)}) copy-start(pred[128]{0:T(512)(128)(4,1)} %copy-done.6) | copy-start | bytes 388
  29.0 31.0 %copy-start.2 = (bf16[1,1608,256]{2,1,0:T(8,128)(2,1)S(1)}, bf16[1,1608,256]{2,1,0:T(8,128)(2,1)}, u32[]{:S(2)}) copy-start(bf16[1,1608,256]{2,1,0:T(8,128)(2,1)} %param.13) | copy-start | bytes 2469892
  76.6 7.3 %copy-start.10 = (f32[128]{0:T(128)S(1)}, f32[128]{0:T(128)}, u32[]{:S(2)}) copy-start(f32[128]{0:T(128)} %broadcast_multiply_fusion.1) | copy-start | bytes 1540
  89.1 121.1 %all-gather.7.cloned.1.call-start = ((), (), s32[]{:S(2)}) async-start(), calls=%async_computation.1 | async-start | bytes 5242880 | tf_op jit(solution)/shard_map/all_gather | solution.py:95
  89.9 189.7 %all-gather.9.cloned.1.call-start = ((), (), s32[]{:S(2)}) async-start(), calls=%async_computation.2 | async-start | bytes 4259840 | tf_op jit(solution)/shard_map/all_gather | solution.py:90
  95.8 236.6 %all-gather.11.cloned.1.call-start = ((), (), s32[]{:S(2)}) async-start(), calls=%async_computation.3 | async-start | bytes 5242880 | tf_op jit(solution)/shard_map/all_gather | solution.py:101
  332.3 14.0 %copy-start.1 = (bf16[128,2048]{1,0:T(8,128)(2,1)S(1)}, bf16[128,2048]{1,0:T(8,128)(2,1)}, u32[]{:S(2)}) copy-start(bf16[128,2048]{1,0:T(8,128)(2,1)} %param.9) | copy-start | bytes 1572868
Sparse Core Ops, SparseCore 0:
  89.2 68.0 all-gather.4
  159.1 51.0 all-gather.6
  211.8 67.7 all-gather.8
  281.3 51.0 all-gather.10
where the time goes:
time: 353 us
  waiting for transfers between devices  224 us (63%)
  blocking collectives  45.9 us (13%)
  matrix products  44.8 us (13%)
  other arithmetic  16.4 us (5%)
  between operations  13.3 us (4%)
  local copies, waits for them, and re-layouts  8.02 us (2%)
    all_gather x1, waiting for transfers between devices, body(): lax.all_gather(key_reduced_precision, 'dp', axis=1, tiled=True)  61 us
    all_gather x1, waiting for transfers between devices, body(): lax.all_gather(value_reduced_precision, 'dp', axis=1, tiled=True)  56.2 us
    all_gather x1, waiting for transfers between devices, body(): lax.all_gather(key_projection_matrix, 'seq', axis=1, tiled=True)  52.9 us
    all_gather x1, waiting for transfers between devices, body(): lax.all_gather(value_projection_matrix, 'seq', axis=1, tiled=True)  52.8 us
    dot_general x1, matrix products, body(): lax.dot_general(value_all, lax.all_gather(value_projection_matrix, 'seq',...  14 us
    dot_general x1, matrix products, body(): lax.dot_general(key_all, lax.all_gather(key_projection_matrix, 'seq', axi...  13.1 us
    all_gather x1, blocking collectives, body(): lax.all_gather(packed_query, 'seq', axis=0, tiled=True)  10.5 us
    pmax x1, blocking collectives, body(): row_top = lax.pmax(jnp.max(scores, axis=-1), 'seq')  9.25 us
  transfers between devices with their start and end apart: 4, of which 4 were waited for; matrix products, arithmetic and copies ran while one was open for 5% of the time, Pallas kernels for 0%

commit v1 on v0

--- a/solution.py
+++ b/solution.py
@@ -1,6 +1,10 @@
+import functools
+
 import jax
 import jax.numpy as jnp
 from jax import lax
+from jax.experimental import pallas as pl
+from jax.experimental.pallas import tpu as pltpu
 from jax.sharding import PartitionSpec as P
 
 QUERY_HEAD_COUNT = 64
@@ -15,7 +19,7 @@
 masked = -1e30
 
 
-def body(
+def body_any(
     queries,
     out_grad,
     token_image,
@@ -105,6 +109,422 @@
     return feature_sum.astype(jnp.bfloat16)[None]
 
 
+MESH = pl.DeviceIdType.MESH
+NT = (((1,), (1,)), ((), ()))
+NN = (((1,), (0,)), ((), ()))
+CHUNK = 272
+FEATURE_TILE = 256
+
+
+def dot(a, b, dims):
+    return lax.dot_general(a, b, dims, preferred_element_type=jnp.float32)
+
+
+def kernel(
+    sizes,
+    image_ref,
+    limit_ref,
+    query_ref,
+    grad_ref,
+    key_ref,
+    value_ref,
+    gain_ref,
+    key_weight_ref,
+    value_weight_ref,
+    out_ref,
+    text,
+    score,
+    grad_prob,
+    stats,
+    rows_all,
+    weights,
+    text_send,
+    text_recv,
+    stat_send,
+    stat_recv,
+    weight_local,
+    weight_send,
+    weight_recv,
+    relay_send,
+    relay_recv,
+    row_send,
+    row_recv,
+):
+    n_seq, n_dp, heads, group = sizes
+    seq = lax.axis_index("seq")
+    img = lax.axis_index("img")
+    dp = lax.axis_index("dp")
+    rows, width = key_ref.shape
+    features = key_weight_ref.shape[0]
+    half = features // 2
+    stack = group * CAP
+    query_rows = n_seq * stack
+    full = rows // CHUNK
+    rest = rows - full * CHUNK
+    padded = rows_all.shape[1]
+    chunks = [(c * CHUNK, CHUNK) for c in range(full)] + [(full * CHUNK, padded - full * CHUNK)]
+    scale = HEAD_WIDTH ** (-0.5)
+    seq_peers = [lax.rem(seq + j, n_seq) for j in range(1, n_seq)]
+
+    own_weights = [
+        pltpu.make_async_copy(
+            ref, weights.at[seq, :, pl.ds(k * width, width)], weight_local.at[k]
+        )
+        for k, ref in enumerate((key_weight_ref, value_weight_ref))
+    ]
+    for copy in own_weights:
+        copy.start()
+
+    barrier = pltpu.get_barrier_semaphore()
+    for peer in seq_peers:
+        pl.semaphore_signal(barrier, inc=1, device_id={"seq": peer}, device_id_type=MESH)
+    pl.semaphore_signal(barrier, inc=1, device_id={"img": 1 - img}, device_id_type=MESH)
+    for j in range(1, n_dp):
+        pl.semaphore_signal(
+            barrier, inc=1, device_id={"dp": lax.rem(dp + j, n_dp)}, device_id_type=MESH
+        )
+
+    tokens = image_ref.shape[1]
+    attends = image_ref[...] == img
+    upper = (
+        lax.broadcasted_iota(jnp.int32, (tokens, tokens), 0)
+        <= lax.broadcasted_iota(jnp.int32, (tokens, tokens), 1)
+    ).astype(jnp.bfloat16)
+    counts = dot(
+        jnp.broadcast_to(attends.astype(jnp.float32), (CAP, tokens)).astype(jnp.bfloat16), upper, NN
+    )
+    slot = lax.broadcasted_iota(jnp.int32, (CAP, tokens), 0).astype(jnp.float32) + 1.0
+    picker = jnp.where(attends & (counts == slot), 1.0, 0.0).astype(jnp.bfloat16)
+    for k, ref in enumerate((query_ref, grad_ref)):
+        packed = dot(picker, ref[...], NN).astype(jnp.bfloat16)
+        for h in range(heads):
+            for g in range(group):
+                column = (h * group + g) * HEAD_WIDTH
+                text[seq, k, h, g * CAP : (g + 1) * CAP, :] = packed[:, column : column + HEAD_WIDTH]
+
+    pl.semaphore_wait(barrier, n_seq - 1 + 1 + n_dp - 1)
+
+    def text_copy(owner, peer, j):
+        return pltpu.make_async_remote_copy(
+            src_ref=text.at[owner],
+            dst_ref=text.at[owner],
+            send_sem=text_send.at[j],
+            recv_sem=text_recv.at[owner],
+            device_id={"seq": peer},
+            device_id_type=MESH,
+        )
+
+    for j, peer in enumerate(seq_peers):
+        text_copy(seq, peer, j).start()
+
+    gain = gain_ref[...]
+    live_limit = limit_ref[0]
+
+    def unit_of(row0, size, h):
+        k = key_ref[pl.ds(row0, size), h * HEAD_WIDTH : (h + 1) * HEAD_WIDTH].astype(jnp.float32)
+        inverse = lax.rsqrt(jnp.mean(k * k, axis=-1, keepdims=True) + epsilon)
+        return k * inverse, inverse
+
+    for j, peer in enumerate(seq_peers):
+        text_copy(peer, peer, j).wait_recv()
+
+    def heads_of(k, h):
+        return text[:, k, h].reshape(query_rows, HEAD_WIDTH)
+
+    def first_pass(row0, size, tops):
+        new_tops = []
+        local = row0 + lax.broadcasted_iota(jnp.int32, (size, 1), 0)
+        row = seq * rows + local
+        live = (row // TILE_ROWS < live_limit) & (row % TILE_ROWS < TILE_TOK)
+        for h in range(heads):
+            unit, _ = unit_of(row0, size, h)
+            normed = (unit * gain).astype(jnp.bfloat16)
+            s = jnp.where(live, dot(normed, heads_of(0, h), NT) * scale, masked)
+            score[h, pl.ds(row0, size), :] = s
+            new_tops.append(jnp.maximum(tops[h], jnp.max(s, axis=0, keepdims=True)))
+        return tuple(new_tops)
+
+    tops = tuple(jnp.full((1, query_rows), masked, jnp.float32) for _ in range(heads))
+    tops = lax.fori_loop(
+        0, full, lambda i, c: first_pass(pl.multiple_of(i * CHUNK, 16), CHUNK, c), tops
+    )
+    tops = first_pass(full * CHUNK, rest, tops)
+
+    def second_pass(row0, size, sums):
+        new_sums = []
+        for h in range(heads):
+            e = jnp.exp(score[h, pl.ds(row0, size), :] - tops[h])
+            v = value_ref[pl.ds(row0, size), h * HEAD_WIDTH : (h + 1) * HEAD_WIDTH]
+            p = dot(v, heads_of(1, h), NT)
+            score[h, pl.ds(row0, size), :] = e
+            grad_prob[h, pl.ds(row0, size), :] = p
+            new_sums.append(sums[2 * h] + jnp.sum(e, axis=0, keepdims=True))
+            new_sums.append(sums[2 * h + 1] + jnp.sum(e * p, axis=0, keepdims=True))
+        return tuple(new_sums)
+
+    sums = tuple(jnp.zeros((1, query_rows), jnp.float32) for _ in range(2 * heads))
+    sums = lax.fori_loop(
+        0, full, lambda i, c: second_pass(pl.multiple_of(i * CHUNK, 16), CHUNK, c), sums
+    )
+    sums = second_pass(full * CHUNK, rest, sums)
+    for h in range(heads):
+        columns = slice(h * query_rows, (h + 1) * query_rows)
+        stats[seq, 0:1, columns] = tops[h]
+        stats[seq, 1:2, columns] = sums[2 * h]
+        stats[seq, 2:3, columns] = sums[2 * h + 1]
+        stats[seq, 3:8, columns] = jnp.zeros((5, query_rows), jnp.float32)
+
+    def stat_copy(owner, peer, j):
+        return pltpu.make_async_remote_copy(
+            src_ref=stats.at[owner],
+            dst_ref=stats.at[owner],
+            send_sem=stat_send.at[j],
+            recv_sem=stat_recv.at[owner],
+            device_id={"seq": peer},
+            device_id_type=MESH,
+        )
+
+    for j, peer in enumerate(seq_peers):
+        stat_copy(seq, peer, j).start()
+    for copy in own_weights:
+        copy.wait()
+    for j, peer in enumerate(seq_peers):
+        stat_copy(peer, peer, j).wait_recv()
+
+    def weight_copy(owner, peer, j):
+        part = weights.at[owner, pl.ds(pl.multiple_of(img * half, half), half)]
+        return pltpu.make_async_remote_copy(
+            src_ref=part,
+            dst_ref=part,
+            send_sem=weight_send.at[j],
+            recv_sem=weight_recv.at[owner],
+            device_id={"seq": peer},
+            device_id_type=MESH,
+        )
+
+    def relay_copy(owner, j, which):
+        part = weights.at[owner, pl.ds(pl.multiple_of(which * half, half), half)]
+        return pltpu.make_async_remote_copy(
+            src_ref=part,
+            dst_ref=part,
+            send_sem=relay_send.at[j],
+            recv_sem=relay_recv.at[owner],
+            device_id={"img": 1 - img},
+            device_id_type=MESH,
+        )
+
+    for j, peer in enumerate(seq_peers):
+        weight_copy(seq, peer, j).start()
+
+    all_tops = [stats[i, 0:1, :] for i in range(n_seq)]
+    top = functools.reduce(jnp.maximum, all_tops)
+    factors = [jnp.exp(t - top) for t in all_tops]
+    total = sum(f * stats[i, 1:2, :] for i, f in enumerate(factors))
+    inner_all = sum(f * stats[i, 2:3, :] for i, f in enumerate(factors)) / total
+    own_factor_all = jnp.exp(stats[seq, 0:1, :] - top) / total
+
+    def row_copy(owner, row0, size, c, side, distance):
+        part = rows_all.at[owner, pl.ds(row0, size)]
+        return pltpu.make_async_remote_copy(
+            src_ref=part,
+            dst_ref=part,
+            send_sem=row_send.at[side, distance, c],
+            recv_sem=row_recv.at[owner, c],
+            device_id={"dp": dp + 1 if side == 0 else dp - 1},
+            device_id_type=MESH,
+        )
+
+    def forward(row0, size, c, distance, act):
+        for side in range(2):
+            owner = dp - distance if side == 0 else dp + distance
+            if side == 0:
+                sends = (owner >= 0) & (dp < n_dp - 1)
+            else:
+                sends = (owner < n_dp) & (dp > 0)
+
+            @pl.when(sends)
+            def _():
+                act(row_copy(owner, row0, size, c, side, distance))
+
+    def arrive(row0, size, c, distance):
+        for side in range(2):
+            owner = dp - distance if side == 0 else dp + distance
+
+            @pl.when((owner >= 0) & (owner < n_dp))
+            def _():
+                row_copy(owner, row0, size, c, side, 0).wait_recv()
+
+    def third_pass(row0, size):
+        for h in range(heads):
+            columns = slice(h * query_rows, (h + 1) * query_rows)
+            p = score[h, pl.ds(row0, size), :] * own_factor_all[:, columns]
+            g = (p * (grad_prob[h, pl.ds(row0, size), :] - inner_all[:, columns])).astype(jnp.bfloat16)
+            value_gradient = dot(p.astype(jnp.bfloat16), heads_of(1, h), NN)
+            unit_grad = dot(g, heads_of(0, h), NN) * scale * gain
+            unit, inverse = unit_of(row0, size, h)
+            key_gradient = inverse * (
+                unit_grad - unit * jnp.mean(unit_grad * unit, axis=-1, keepdims=True)
+            )
+            lane = h * HEAD_WIDTH
+            rows_all[dp, pl.ds(row0, size), lane : lane + HEAD_WIDTH] = key_gradient.astype(
+                jnp.bfloat16
+            )
+            lane = lane + width
+            rows_all[dp, pl.ds(row0, size), lane : lane + HEAD_WIDTH] = value_gradient.astype(
+                jnp.bfloat16
+            )
+
+    def start(copy):
+        copy.start()
+
+    def own_chunk(i, _):
+        row0 = pl.multiple_of(i * CHUNK, 16)
+        third_pass(row0, CHUNK)
+        forward(row0, CHUNK, i, 0, start)
+        return 0
+
+    lax.fori_loop(0, full, own_chunk, 0)
+    third_pass(full * CHUNK, rest)
+    forward(chunks[-1][0], chunks[-1][1], full, 0, start)
+
+    for c, (row0, size) in enumerate(chunks):
+        arrive(row0, size, c, 1)
+        forward(row0, size, c, 1, start)
+    for j, peer in enumerate(seq_peers):
+        weight_copy(peer, peer, j).wait_recv()
+        relay_copy(peer, j, img).start()
+    for c, (row0, size) in enumerate(chunks):
+        arrive(row0, size, c, 2)
+        forward(row0, size, c, 2, start)
+    for j, peer in enumerate(seq_peers):
+        relay_copy(peer, j, 1 - img).wait_recv()
+
+    def multiply(row0, size):
+        def tile(i, _):
+            column = pl.multiple_of(i * FEATURE_TILE, FEATURE_TILE)
+            total = functools.reduce(
+                jnp.add,
+                [
+                    dot(
+                        rows_all[b, pl.ds(row0, size), :],
+                        weights[b, pl.ds(column, FEATURE_TILE), :],
+                        NT,
+                    )
+                    for b in range(n_dp)
+                ],
+            )
+            out_ref[pl.ds(row0, size), pl.ds(column, FEATURE_TILE)] = total.astype(out_ref.dtype)
+            return 0
+
+        lax.fori_loop(0, features // FEATURE_TILE, tile, 0)
+
+    def finish_chunk(i, _):
+        row0 = pl.multiple_of(i * CHUNK, 16)
+        arrive(row0, CHUNK, i, 3)
+        multiply(row0, CHUNK)
+        return 0
+
+    lax.fori_loop(0, full, finish_chunk, 0)
+    arrive(chunks[-1][0], chunks[-1][1], full, 3)
+    multiply(full * CHUNK, rest)
+
+    def sent(copy):
+        copy.wait_send()
+
+    for c, (row0, size) in enumerate(chunks):
+        for distance in range(n_dp - 1):
+            forward(row0, size, c, distance, sent)
+    for j, peer in enumerate(seq_peers):
+        text_copy(seq, peer, j).wait_send()
+        stat_copy(seq, peer, j).wait_send()
+        weight_copy(seq, peer, j).wait_send()
+        relay_copy(peer, j, img).wait_send()
+
+
+def body_kernel(
+    sizes,
+    queries,
+    out_grad,
+    token_image,
+    unnormed_keys,
+    values,
+    key_gain,
+    tile_count,
+    key_projection_matrix,
+    value_projection_matrix,
+):
+    n_seq, n_dp, heads, group = sizes
+    rows, width = unnormed_keys.shape[1:]
+    features = key_projection_matrix.shape[0]
+    query_rows = n_seq * group * CAP
+    chunk_count = rows // CHUNK + 1
+    padded = -(-rows // 16) * 16
+    tile_limit = lax.dynamic_slice_in_dim(tile_count, lax.axis_index("img"), 1)
+    vmem = pl.BlockSpec(memory_space=pltpu.VMEM)
+    anywhere = pl.BlockSpec(memory_space=pl.ANY)
+    dma = pltpu.SemaphoreType.DMA
+    result = pl.pallas_call(
+        functools.partial(kernel, sizes),
+        out_shape=jax.ShapeDtypeStruct((rows, features), jnp.bfloat16),
+        in_specs=[
+            vmem,
+            pl.BlockSpec(memory_space=pltpu.SMEM),
+            vmem,
+            vmem,
+            vmem,
+            vmem,
+            vmem,
+            anywhere,
+            anywhere,
+        ],
+        out_specs=vmem,
+        scratch_shapes=[
+            pltpu.VMEM((n_seq, 2, heads, group * CAP, HEAD_WIDTH), jnp.bfloat16),
+            pltpu.VMEM((heads, rows, query_rows), jnp.float32),
+            pltpu.VMEM((heads, rows, query_rows), jnp.float32),
+            pltpu.VMEM((n_seq, 8, heads * query_rows), jnp.float32),
+            pltpu.VMEM((n_dp, padded, 2 * width), jnp.bfloat16),
+            pltpu.VMEM((n_seq, features, 2 * width), jnp.bfloat16),
+            dma((n_seq - 1,)),
+            dma((n_seq,)),
+            dma((n_seq - 1,)),
+            dma((n_seq,)),
+            dma((2,)),
+            dma((n_seq - 1,)),
+            dma((n_seq,)),
+            dma((n_seq - 1,)),
+            dma((n_seq,)),
+            dma((2, n_dp - 1, chunk_count)),
+            dma((n_dp, chunk_count)),
+        ],
+        compiler_params=pltpu.CompilerParams(
+            collective_id=0, has_side_effects=True, vmem_limit_bytes=60 * 1024 * 1024
+        ),
+    )(
+        token_image[None],
+        tile_limit,
+        queries,
+        out_grad,
+        unnormed_keys[0],
+        values[0],
+        key_gain[None],
+        key_projection_matrix,
+        value_projection_matrix,
+    )
+    return result[None]
+
+
+def body(*args):
+    n_seq, n_img, n_dp = (lax.axis_size(name) for name in ("seq", "img", "dp"))
+    rows, width = args[3].shape[1:]
+    heads = width // HEAD_WIDTH
+    group = args[0].shape[1] // width
+    fits = n_img == 2 and n_seq == n_dp == 4 and args[7].shape[1] == width and rows % 8 == 0
+    if fits and rows % CHUNK and rows % CHUNK % 16 == 8:
+        return body_kernel((n_seq, n_dp, heads, group), *args)
+    return body_any(*args)
+
+
 def solution(mesh):
     in_specs = (
         P("seq", "dp"),

time: 353 us -> 147 us (0.42)
  waiting for transfers between devices: 224 us -> 0 us
  Pallas kernels: 0 us -> 138 us
  blocking collectives: 45.9 us -> 0 us
  matrix products: 44.8 us -> 0 us
  other arithmetic: 16.4 us -> 0 us
  between operations: 13.3 us -> 0.01 us
    all_gather x4 -> x0, waiting for transfers between devices: 223 us -> none  [the longest x1 61 us: body(): lax.all_gather(key_reduced_precision, 'dp', axis=1, tiled=True)]
    pallas_call x0 -> x1, Pallas kernels: none -> 138 us  [body_kernel(): pl.pallas_call(functools.partial(kernel, sizes), out_shape=jax.ShapeDtype...]
    dot_general x8 -> x0, matrix products: 44.8 us -> none  [the longest x1 14 us: body(): lax.dot_general(value_all, lax.all_gather(value_projection_matrix, 'seq',...]
    all_gather x2 -> x0, blocking collectives: 18.5 us -> none  [the longest x1 10.5 us: body(): lax.all_gather(packed_query, 'seq', axis=0, tiled=True)]
    psum x2 -> x0, blocking collectives: 18.1 us -> none  [the longest x1 9.06 us: body(): row_total = lax.psum(jnp.sum(exponent, axis=-1), 'seq')]
    pmax x1 -> x0, blocking collectives: 9.25 us -> none  [body(): row_top = lax.pmax(jnp.max(scores, axis=-1), 'seq')]
    convert_element_type x2 -> x0, other arithmetic: 8.27 us -> none  [the longest x1 7.24 us: body(): probs_low = probabilities.astype(jnp.bfloat16)]
    unnamed x26 -> x1, local copies, waits for them, and re-layouts: 0.12 us -> 6.87 us
  transfers between devices with their start and end apart: 4 -> 0, of which waited for: 4 -> 0; matrix products, arithmetic and copies ran while one was open for 5% -> 0% of each run, Pallas kernels for 0% -> 0%
where the time goes in v1:
time: 147 us
  Pallas kernels  138 us (94%)
  local copies, waits for them, and re-layouts  8.11 us (6%)
    pallas_call x1, Pallas kernels, body_kernel(): pl.pallas_call(functools.partial(kernel, sizes), out_shape=jax.ShapeDtype...  138 us
    unnamed x1, local copies, waits for them, and re-layouts  6.87 us

profile of v1, /device:TPU:0, one launch (start us, length us, event | category | flops | bytes accessed | tf_op | source)
XLA Modules:
  0.0 146.5 jit_solution(18233826683966708696)
XLA Ops:
  0.0 1.2 dynamic_slice.3.limit_ref
  1.2 138.4 %shard_map.91 = bf16[1608,2048]{1,0:T(8,128)(2,1)} custom-call(s32[1,128]{1,0:T(1,128)} %bitcast.8, s32[1]{0:T(128)} %dynamic_slice.3.limit_ref, bf16[128,2048]{1,0:T(8,128)(2,1)} %query_ref.1, bf16[128,2048]{1,0:T(8,128)(2,1)} %grad_ref.1, bf16[1608,256]{1,0:T(8,128)(2,1)} %bitcast.6, bf16[1608,256]{1,0:T(8,128)(2,1)} %bitcast.7, f32[1,128]{1,0:T(1,128)} %bitcast.9, ...), custom_call_target="tpu_custom_call" | custom-call | tf_op jit(solution)/shard_map/pallas_call | solution.py:466
  139.6 6.9 %copy.11 = bf16[1,1608,2048]{2,1,0:T(8,128)(2,1)} copy(bf16[1,1608,2048]{2,1,0:T(8,128)(2,1)} %bitcast.5) | data formatting | bytes 13172736

commit v2 on v1

--- a/solution.py
+++ b/solution.py
@@ -218,7 +218,7 @@
         text_copy(seq, peer, j).start()
 
     gain = gain_ref[...]
-    live_limit = limit_ref[0]
+    live_limit = limit_ref[img]
 
     def unit_of(row0, size, h):
         k = key_ref[pl.ds(row0, size), h * HEAD_WIDTH : (h + 1) * HEAD_WIDTH].astype(jnp.float32)
@@ -459,13 +459,12 @@
     query_rows = n_seq * group * CAP
     chunk_count = rows // CHUNK + 1
     padded = -(-rows // 16) * 16
-    tile_limit = lax.dynamic_slice_in_dim(tile_count, lax.axis_index("img"), 1)
     vmem = pl.BlockSpec(memory_space=pltpu.VMEM)
-    anywhere = pl.BlockSpec(memory_space=pl.ANY)
+    anywhere = pl.BlockSpec(memory_space=pltpu.HBM)
     dma = pltpu.SemaphoreType.DMA
     result = pl.pallas_call(
         functools.partial(kernel, sizes),
-        out_shape=jax.ShapeDtypeStruct((rows, features), jnp.bfloat16),
+        out_shape=pltpu.VMEM((rows, features), jnp.bfloat16),
         in_specs=[
             vmem,
             pl.BlockSpec(memory_space=pltpu.SMEM),
@@ -498,11 +497,11 @@
             dma((n_dp, chunk_count)),
         ],
         compiler_params=pltpu.CompilerParams(
-            collective_id=0, has_side_effects=True, vmem_limit_bytes=60 * 1024 * 1024
+            collective_id=0, has_side_effects=True, vmem_limit_bytes=40 * 1024 * 1024
         ),
     )(
         token_image[None],
-        tile_limit,
+        tile_count,
         queries,
         out_grad,
         unnormed_keys[0],

time: 147 us -> 146 us (level)
  Pallas kernels: 138 us -> 134 us
  local copies, waits for them, and re-layouts: 8.11 us -> 11.6 us
    unnamed x1 -> x19, local copies, waits for them, and re-layouts: 6.87 us -> 11.6 us
    pallas_call x1, Pallas kernels: 138 us -> 134 us  [body_kernel(): pl.pallas_call(functools.partial(kernel, sizes), out_shape=pltpu.VMEM((ro...]
where the time goes in v2:
time: 146 us
  Pallas kernels  134 us (92%)
  local copies, waits for them, and re-layouts  11.6 us (8%)
    pallas_call x1, Pallas kernels, body_kernel(): pl.pallas_call(functools.partial(kernel, sizes), out_shape=pltpu.VMEM((ro...  134 us
    unnamed x19, local copies, waits for them, and re-layouts  11.6 us

profile of v2, /device:TPU:0, one launch (start us, length us, event | category | flops | bytes accessed | tf_op | source)
XLA Modules:
  0.0 145.6 jit_solution(13461220830710660666)
XLA Ops:
  0.0 0.0 copy-start
  0.0 1.2 copy-done
  1.2 0.0 copy-start.1
  1.2 1.2 copy-done.1
  2.5 0.0 copy-start.2
  2.5 1.1 copy-done.2
  3.6 0.0 copy-start.3
  3.6 1.1 copy-done.3
  4.7 0.0 copy-start.4
  4.7 1.0 copy-done.4
  5.8 0.0 copy-start.5
  5.8 1.0 copy-done.5
  6.8 0.0 copy-start.6
  6.8 0.7 copy-done.6
  7.5 0.0 copy-start.7
  7.5 0.7 copy-done.7
  8.1 0.0 copy-start.8
  8.1 0.7 copy-done.8
  8.8 134.0 %shard_map.91 = bf16[1608,2048]{1,0:T(8,128)(2,1)S(1)} custom-call(s32[1,128]{1,0:T(1,128)S(1)} %bitcast.8, s32[2]{0:T(128)S(1)} %copy-done.7, bf16[128,2048]{1,0:T(8,128)(2,1)S(1)} %copy-done.4, bf16[128,2048]{1,0:T(8,128)(2,1)S(1)} %copy-done.5, bf16[1608,256]{1,0:T(8,128)(2,1)S(1)} %bitcast.6, bf16[1608,256]{1,0:T(8,128)(2,1)S(1)} %bitcast.7, ...), custom_call_target="tpu_custom_call" | custom-call | tf_op jit(solution)/shard_map/pallas_call | solution.py:465
  142.8 2.8 %copy.11 = bf16[1,1608,2048]{2,1,0:T(8,128)(2,1)} copy(bf16[1,1608,2048]{2,1,0:T(8,128)(2,1)S(1)} %bitcast.5) | data formatting | bytes 13172736
Async XLA Ops:
  0.0 1.2 copy-start
  1.2 1.2 copy-start.1
  2.5 1.1 copy-start.2
  3.6 1.1 copy-start.3
  4.7 1.0 copy-start.4
  5.8 1.0 copy-start.5
  6.8 0.7 copy-start.6
  7.5 0.7 copy-start.7
  8.1 0.7 copy-start.8

commit v3 on v2

--- a/solution.py
+++ b/solution.py
@@ -114,6 +114,7 @@
 NN = (((1,), (0,)), ((), ()))
 CHUNK = 272
 FEATURE_TILE = 256
+VMEM_BYTES = 67043328
 
 
 def dot(a, b, dims):
@@ -124,20 +125,26 @@
     sizes,
     image_ref,
     limit_ref,
+    query_hbm,
+    grad_hbm,
+    key_hbm,
+    value_hbm,
+    gain_ref,
+    key_weight_ref,
+    value_weight_ref,
+    out_ref,
     query_ref,
     grad_ref,
     key_ref,
     value_ref,
-    gain_ref,
-    key_weight_ref,
-    value_weight_ref,
-    out_ref,
+    normed_ref,
     text,
     score,
     grad_prob,
     stats,
     rows_all,
     weights,
+    load_sem,
     text_send,
     text_recv,
     stat_send,
@@ -164,7 +171,22 @@
     padded = rows_all.shape[1]
     chunks = [(c * CHUNK, CHUNK) for c in range(full)] + [(full * CHUNK, padded - full * CHUNK)]
     scale = HEAD_WIDTH ** (-0.5)
-    seq_peers = [lax.rem(seq + j, n_seq) for j in range(1, n_seq)]
+    near, far = seq % 2, seq // 2
+    seq_peers = [far * 2 + 1 - near, (1 - far) * 2 + near, (1 - far) * 2 + 1 - near]
+
+    loads = [
+        pltpu.make_async_copy(source, target, load_sem.at[k])
+        for k, (source, target) in enumerate(
+            (
+                (query_hbm, query_ref),
+                (grad_hbm, grad_ref),
+                (key_hbm, key_ref),
+                (value_hbm, value_ref),
+            )
+        )
+    ]
+    for copy in loads:
+        copy.start()
 
     own_weights = [
         pltpu.make_async_copy(
@@ -172,9 +194,6 @@
         )
         for k, ref in enumerate((key_weight_ref, value_weight_ref))
     ]
-    for copy in own_weights:
-        copy.start()
-
     barrier = pltpu.get_barrier_semaphore()
     for peer in seq_peers:
         pl.semaphore_signal(barrier, inc=1, device_id={"seq": peer}, device_id_type=MESH)
@@ -196,6 +215,7 @@
     slot = lax.broadcasted_iota(jnp.int32, (CAP, tokens), 0).astype(jnp.float32) + 1.0
     picker = jnp.where(attends & (counts == slot), 1.0, 0.0).astype(jnp.bfloat16)
     for k, ref in enumerate((query_ref, grad_ref)):
+        loads[k].wait()
         packed = dot(picker, ref[...], NN).astype(jnp.bfloat16)
         for h in range(heads):
             for g in range(group):
@@ -225,54 +245,74 @@
         inverse = lax.rsqrt(jnp.mean(k * k, axis=-1, keepdims=True) + epsilon)
         return k * inverse, inverse
 
-    for j, peer in enumerate(seq_peers):
-        text_copy(peer, peer, j).wait_recv()
-
     def heads_of(k, h):
         return text[:, k, h].reshape(query_rows, HEAD_WIDTH)
 
-    def first_pass(row0, size, tops):
-        new_tops = []
-        local = row0 + lax.broadcasted_iota(jnp.int32, (size, 1), 0)
-        row = seq * rows + local
-        live = (row // TILE_ROWS < live_limit) & (row % TILE_ROWS < TILE_TOK)
+    for copy in own_weights:
+        copy.start()
+    for copy in loads[2:]:
+        copy.wait()
+
+    def normalize(row0, size):
         for h in range(heads):
             unit, _ = unit_of(row0, size, h)
-            normed = (unit * gain).astype(jnp.bfloat16)
-            s = jnp.where(live, dot(normed, heads_of(0, h), NT) * scale, masked)
-            score[h, pl.ds(row0, size), :] = s
-            new_tops.append(jnp.maximum(tops[h], jnp.max(s, axis=0, keepdims=True)))
-        return tuple(new_tops)
-
-    tops = tuple(jnp.full((1, query_rows), masked, jnp.float32) for _ in range(heads))
-    tops = lax.fori_loop(
-        0, full, lambda i, c: first_pass(pl.multiple_of(i * CHUNK, 16), CHUNK, c), tops
-    )
-    tops = first_pass(full * CHUNK, rest, tops)
-
-    def second_pass(row0, size, sums):
-        new_sums = []
+            normed_ref[pl.ds(row0, size), h * HEAD_WIDTH : (h + 1) * HEAD_WIDTH] = (
+                unit * gain
+            ).astype(jnp.bfloat16)
+
+    def over_chunks(act, carry):
+        carry = lax.fori_loop(
+            0, full, lambda i, c: act(pl.multiple_of(i * CHUNK, 16), CHUNK, c), carry
+        )
+        return act(full * CHUNK, rest, carry)
+
+    def normalize_chunk(row0, size, carry):
+        normalize(row0, size)
+        return carry
+
+    over_chunks(normalize_chunk, 0)
+
+    for j, owner in enumerate([seq] + seq_peers):
+        if j:
+            text_copy(owner, owner, j - 1).wait_recv()
+        lanes = pl.ds(pl.multiple_of(owner * stack, stack), stack)
+
+        def first_pass(row0, size, tops):
+            new_tops = []
+            row = seq * rows + row0 + lax.broadcasted_iota(jnp.int32, (size, 1), 0)
+            live = (row // TILE_ROWS < live_limit) & (row % TILE_ROWS < TILE_TOK)
+            for h in range(heads):
+                normed = normed_ref[pl.ds(row0, size), h * HEAD_WIDTH : (h + 1) * HEAD_WIDTH]
+                s = jnp.where(live, dot(normed, text[owner, 0, h], NT) * scale, masked)
+                score[h, pl.ds(row0, size), lanes] = s
+                new_tops.append(jnp.maximum(tops[h], jnp.max(s, axis=0, keepdims=True)))
+            return tuple(new_tops)
+
+        tops = over_chunks(
+            first_pass, tuple(jnp.full((1, stack), masked, jnp.float32) for _ in range(heads))
+        )
+
+        def second_pass(row0, size, sums):
+            new_sums = []
+            for h in range(heads):
+                e = jnp.exp(score[h, pl.ds(row0, size), lanes] - tops[h])
+                v = value_ref[pl.ds(row0, size), h * HEAD_WIDTH : (h + 1) * HEAD_WIDTH]
+                p = dot(v, text[owner, 1, h], NT)
+                score[h, pl.ds(row0, size), lanes] = e
+                grad_prob[h, pl.ds(row0, size), lanes] = p
+                new_sums.append(sums[2 * h] + jnp.sum(e, axis=0, keepdims=True))
+                new_sums.append(sums[2 * h + 1] + jnp.sum(e * p, axis=0, keepdims=True))
+            return tuple(new_sums)
+
+        sums = over_chunks(
+            second_pass, tuple(jnp.zeros((1, stack), jnp.float32) for _ in range(2 * heads))
+        )
         for h in range(heads):
-            e = jnp.exp(score[h, pl.ds(row0, size), :] - tops[h])
-            v = value_ref[pl.ds(row0, size), h * HEAD_WIDTH : (h + 1) * HEAD_WIDTH]
-            p = dot(v, heads_of(1, h), NT)
-            score[h, pl.ds(row0, size), :] = e
-            grad_prob[h, pl.ds(row0, size), :] = p
-            new_sums.append(sums[2 * h] + jnp.sum(e, axis=0, keepdims=True))
-            new_sums.append(sums[2 * h + 1] + jnp.sum(e * p, axis=0, keepdims=True))
-        return tuple(new_sums)
-
-    sums = tuple(jnp.zeros((1, query_rows), jnp.float32) for _ in range(2 * heads))
-    sums = lax.fori_loop(
-        0, full, lambda i, c: second_pass(pl.multiple_of(i * CHUNK, 16), CHUNK, c), sums
-    )
-    sums = second_pass(full * CHUNK, rest, sums)
-    for h in range(heads):
-        columns = slice(h * query_rows, (h + 1) * query_rows)
-        stats[seq, 0:1, columns] = tops[h]
-        stats[seq, 1:2, columns] = sums[2 * h]
-        stats[seq, 2:3, columns] = sums[2 * h + 1]
-        stats[seq, 3:8, columns] = jnp.zeros((5, query_rows), jnp.float32)
+            columns = pl.ds(pl.multiple_of(h * query_rows + owner * stack, stack), stack)
+            stats[seq, 0:1, columns] = tops[h]
+            stats[seq, 1:2, columns] = sums[2 * h]
+            stats[seq, 2:3, columns] = sums[2 * h + 1]
+    stats[seq, 3:8, :] = jnp.zeros((5, heads * query_rows), jnp.float32)
 
     def stat_copy(owner, peer, j):
         return pltpu.make_async_remote_copy(
@@ -468,22 +508,28 @@
         in_specs=[
             vmem,
             pl.BlockSpec(memory_space=pltpu.SMEM),
-            vmem,
-            vmem,
-            vmem,
-            vmem,
+            anywhere,
+            anywhere,
+            anywhere,
+            anywhere,
             vmem,
             anywhere,
             anywhere,
         ],
         out_specs=vmem,
         scratch_shapes=[
+            pltpu.VMEM(queries.shape, jnp.bfloat16),
+            pltpu.VMEM(queries.shape, jnp.bfloat16),
+            pltpu.VMEM((rows, width), jnp.bfloat16),
+            pltpu.VMEM((rows, width), jnp.bfloat16),
+            pltpu.VMEM((rows, width), jnp.bfloat16),
             pltpu.VMEM((n_seq, 2, heads, group * CAP, HEAD_WIDTH), jnp.bfloat16),
             pltpu.VMEM((heads, rows, query_rows), jnp.float32),
             pltpu.VMEM((heads, rows, query_rows), jnp.float32),
             pltpu.VMEM((n_seq, 8, heads * query_rows), jnp.float32),
             pltpu.VMEM((n_dp, padded, 2 * width), jnp.bfloat16),
             pltpu.VMEM((n_seq, features, 2 * width), jnp.bfloat16),
+            dma((4,)),
             dma((n_seq - 1,)),
             dma((n_seq,)),
             dma((n_seq - 1,)),
@@ -497,7 +543,7 @@
             dma((n_dp, chunk_count)),
         ],
         compiler_params=pltpu.CompilerParams(
-            collective_id=0, has_side_effects=True, vmem_limit_bytes=40 * 1024 * 1024
+            collective_id=0, has_side_effects=True, vmem_limit_bytes=VMEM_BYTES - 2 * rows * features
         ),
     )(
         token_image[None],

time: 146 us -> 140 us (0.959)
  local copies, waits for them, and re-layouts: 11.6 us -> 2.8 us
  Pallas kernels: 134 us -> 137 us
    unnamed x19 -> x1, local copies, waits for them, and re-layouts: 11.6 us -> 2.8 us
    pallas_call x1, Pallas kernels: 134 us -> 137 us  [body_kernel(): pl.pallas_call(functools.partial(kernel, sizes), out_shape=pltpu.VMEM((ro...]
where the time goes in v3:
time: 140 us; the launch traced here: 139 us
  Pallas kernels  137 us (98%)
  local copies, waits for them, and re-layouts  2.8 us (2%)
    pallas_call x1, Pallas kernels, body_kernel(): pl.pallas_call(functools.partial(kernel, sizes), out_shape=pltpu.VMEM((ro...  137 us
    unnamed x1, local copies, waits for them, and re-layouts  2.8 us

profile of v3, /device:TPU:0, one launch (start us, length us, event | category | flops | bytes accessed | tf_op | source)
XLA Modules:
  0.0 139.4 jit_solution(12486416997929048349)
XLA Ops:
  0.0 136.6 %shard_map.91 = bf16[1608,2048]{1,0:T(8,128)(2,1)S(1)} custom-call(s32[1,128]{1,0:T(1,128)} %bitcast.8, s32[2]{0:T(128)} %limit_ref.1, bf16[128,2048]{1,0:T(8,128)(2,1)} %query_hbm.1, bf16[128,2048]{1,0:T(8,128)(2,1)} %grad_hbm.1, bf16[1608,256]{1,0:T(8,128)(2,1)} %bitcast.6, bf16[1608,256]{1,0:T(8,128)(2,1)} %bitcast.7, f32[1,128]{1,0:T(1,128)} %bitcast.9, ...), custom_call_target="tpu_custom_call" | custom-call | tf_op jit(solution)/shard_map/pallas_call | solution.py:505
  136.6 2.8 %copy.11 = bf16[1,1608,2048]{2,1,0:T(8,128)(2,1)} copy(bf16[1,1608,2048]{2,1,0:T(8,128)(2,1)S(1)} %bitcast.5) | data formatting | bytes 13172736

commit v4 on v3

--- a/solution.py
+++ b/solution.py
@@ -112,13 +112,45 @@
 MESH = pl.DeviceIdType.MESH
 NT = (((1,), (1,)), ((), ()))
 NN = (((1,), (0,)), ((), ()))
-CHUNK = 272
+CHUNK = 240
 FEATURE_TILE = 256
 VMEM_BYTES = 67043328
 
 
 def dot(a, b, dims):
     return lax.dot_general(a, b, dims, preferred_element_type=jnp.float32)
+
+
+def multiply(rows_all, weights, row0, size, out_ref, out_row0):
+    def tile(i, _):
+        column = pl.multiple_of(i * FEATURE_TILE, FEATURE_TILE)
+        total = functools.reduce(
+            jnp.add,
+            [
+                dot(
+                    rows_all[b, pl.ds(row0, size), :],
+                    weights[b, pl.ds(column, FEATURE_TILE), :],
+                    NT,
+                )
+                for b in range(rows_all.shape[0])
+            ],
+        )
+        out_ref[pl.ds(out_row0, size), pl.ds(column, FEATURE_TILE)] = total.astype(out_ref.dtype)
+        return 0
+
+    lax.fori_loop(0, weights.shape[1] // FEATURE_TILE, tile, 0)
+
+
+def finish_kernel(done_ref, rows_all, weights, out_ref, last_ref, sems):
+    done = done_ref.shape[0]
+    rest = last_ref.shape[0]
+    first = pltpu.make_async_copy(done_ref, out_ref.at[pl.ds(0, done)], sems.at[0])
+    first.start()
+    multiply(rows_all, weights, done, rest, last_ref, 0)
+    second = pltpu.make_async_copy(last_ref, out_ref.at[pl.ds(done, rest)], sems.at[1])
+    second.start()
+    first.wait()
+    second.wait()
 
 
 def kernel(
@@ -133,6 +165,8 @@
     key_weight_ref,
     value_weight_ref,
     out_ref,
+    rows_all,
+    weights,
     query_ref,
     grad_ref,
     key_ref,
@@ -142,8 +176,6 @@
     score,
     grad_prob,
     stats,
-    rows_all,
-    weights,
     load_sem,
     text_send,
     text_recv,
@@ -439,34 +471,14 @@
     for j, peer in enumerate(seq_peers):
         relay_copy(peer, j, 1 - img).wait_recv()
 
-    def multiply(row0, size):
-        def tile(i, _):
-            column = pl.multiple_of(i * FEATURE_TILE, FEATURE_TILE)
-            total = functools.reduce(
-                jnp.add,
-                [
-                    dot(
-                        rows_all[b, pl.ds(row0, size), :],
-                        weights[b, pl.ds(column, FEATURE_TILE), :],
-                        NT,
-                    )
-                    for b in range(n_dp)
-                ],
-            )
-            out_ref[pl.ds(row0, size), pl.ds(column, FEATURE_TILE)] = total.astype(out_ref.dtype)
-            return 0
-
-        lax.fori_loop(0, features // FEATURE_TILE, tile, 0)
-
     def finish_chunk(i, _):
         row0 = pl.multiple_of(i * CHUNK, 16)
         arrive(row0, CHUNK, i, 3)
-        multiply(row0, CHUNK)
+        multiply(rows_all, weights, row0, CHUNK, out_ref, row0)
         return 0
 
     lax.fori_loop(0, full, finish_chunk, 0)
     arrive(chunks[-1][0], chunks[-1][1], full, 3)
-    multiply(full * CHUNK, rest)
 
     def sent(copy):
         copy.wait_send()
@@ -502,9 +514,15 @@
     vmem = pl.BlockSpec(memory_space=pltpu.VMEM)
     anywhere = pl.BlockSpec(memory_space=pltpu.HBM)
     dma = pltpu.SemaphoreType.DMA
-    result = pl.pallas_call(
+    done = rows // CHUNK * CHUNK
+    kept = 2 * (done * features + n_dp * padded * 2 * width + n_seq * features * 2 * width)
+    finished, rows_all, weights = pl.pallas_call(
         functools.partial(kernel, sizes),
-        out_shape=pltpu.VMEM((rows, features), jnp.bfloat16),
+        out_shape=(
+            pltpu.VMEM((done, features), jnp.bfloat16),
+            pltpu.VMEM((n_dp, padded, 2 * width), jnp.bfloat16),
+            pltpu.VMEM((n_seq, features, 2 * width), jnp.bfloat16),
+        ),
         in_specs=[
             vmem,
             pl.BlockSpec(memory_space=pltpu.SMEM),
@@ -516,7 +534,7 @@
             anywhere,
             anywhere,
         ],
-        out_specs=vmem,
+        out_specs=(vmem, vmem, vmem),
         scratch_shapes=[
             pltpu.VMEM(queries.shape, jnp.bfloat16),
             pltpu.VMEM(queries.shape, jnp.bfloat16),
@@ -527,8 +545,6 @@
             pltpu.VMEM((heads, rows, query_rows), jnp.float32),
             pltpu.VMEM((heads, rows, query_rows), jnp.float32),
             pltpu.VMEM((n_seq, 8, heads * query_rows), jnp.float32),
-            pltpu.VMEM((n_dp, padded, 2 * width), jnp.bfloat16),
-            pltpu.VMEM((n_seq, features, 2 * width), jnp.bfloat16),
             dma((4,)),
             dma((n_seq - 1,)),
             dma((n_seq,)),
@@ -543,7 +559,7 @@
             dma((n_dp, chunk_count)),
         ],
         compiler_params=pltpu.CompilerParams(
-            collective_id=0, has_side_effects=True, vmem_limit_bytes=VMEM_BYTES - 2 * rows * features
+            collective_id=0, has_side_effects=True, vmem_limit_bytes=VMEM_BYTES - kept
         ),
     )(
         token_image[None],
@@ -556,6 +572,14 @@
         key_projection_matrix,
         value_projection_matrix,
     )
+    result = pl.pallas_call(
+        finish_kernel,
+        out_shape=jax.ShapeDtypeStruct((rows, features), jnp.bfloat16),
+        in_specs=[vmem, vmem, vmem],
+        out_specs=pl.BlockSpec(memory_space=pltpu.HBM),
+        scratch_shapes=[pltpu.VMEM((rows - done, features), jnp.bfloat16), dma((2,))],
+        compiler_params=pltpu.CompilerParams(vmem_limit_bytes=8 * 1024 * 1024),
+    )(finished, rows_all, weights)
     return result[None]
 
 

time: 140 us -> 140 us (level)
  Pallas kernels: 137 us -> 140 us
  local copies, waits for them, and re-layouts: 2.8 us -> 0 us
    pallas_call x1 -> x2, Pallas kernels: 137 us -> 140 us  [the longest x1 135 us: body_kernel(): pl.pallas_call(functools.partial(kernel, sizes), out_shape=(pltpu.VMEM((d...]
    unnamed x1 -> x0, local copies, waits for them, and re-layouts: 2.8 us -> none
where the time goes in v4:
time: 140 us
  Pallas kernels  140 us (100%)
    pallas_call x1, Pallas kernels, body_kernel(): pl.pallas_call(functools.partial(kernel, sizes), out_shape=(pltpu.VMEM((d...  135 us
    pallas_call x1, Pallas kernels, body_kernel(): pl.pallas_call(finish_kernel, out_shape=jax.ShapeDtypeStruct((rows, featu...  4.84 us

profile of v4, /device:TPU:0, one launch (start us, length us, event | category | flops | bytes accessed | tf_op | source)
XLA Modules:
  0.0 139.8 jit_solution(9778614176344025528)
XLA Ops:
  0.0 135.0 %shard_map.91 = (bf16[1440,2048]{1,0:T(8,128)(2,1)S(1)}, bf16[4,1616,512]{2,1,0:T(8,128)(2,1)S(1)}, bf16[4,2048,512]{2,1,0:T(8,128)(2,1)S(1)}) custom-call(s32[1,128]{1,0:T(1,128)} %bitcast.7, s32[2]{0:T(128)} %limit_ref.1, bf16[128,2048]{1,0:T(8,128)(2,1)} %query_hbm.1, bf16[128,2048]{1,0:T(8,128)(2,1)} %grad_hbm.1, bf16[1608,256]{1,0:T(8,128)(2,1)} %bitcast.5, ...), custom_call_target="tpu_custom_call" | custom-call | tf_op jit(solution)/shard_map/pallas_call | solution.py:519
  135.0 4.8 %shard_map.92 = bf16[1608,2048]{1,0:T(8,128)(2,1)} custom-call(bf16[1440,2048]{1,0:T(8,128)(2,1)S(1)} %get-tuple-element.8.done_ref, bf16[4,1616,512]{2,1,0:T(8,128)(2,1)S(1)} %get-tuple-element.9.rows_all, bf16[4,2048,512]{2,1,0:T(8,128)(2,1)S(1)} %get-tuple-element.10.weights), custom_call_target="tpu_custom_call" | custom-call | tf_op jit(solution)/shard_map/pallas_call | solution.py:575

commit v5 on v3

--- a/solution.py
+++ b/solution.py
@@ -138,6 +138,7 @@
     key_ref,
     value_ref,
     normed_ref,
+    partial,
     text,
     score,
     grad_prob,
@@ -464,9 +465,33 @@
         multiply(row0, CHUNK)
         return 0
 
+    upper_half = dp // (n_dp // 2)
+    farthest = (n_dp - 1) * (1 - upper_half)
+
+    def last_product(block, column):
+        return dot(
+            rows_all[block, full * CHUNK : rows, :],
+            weights[block, pl.ds(column, FEATURE_TILE), :],
+            NT,
+        )
+
+    def partial_tile(i, _):
+        column = pl.multiple_of(i * FEATURE_TILE, FEATURE_TILE)
+        partial[:, pl.ds(column, FEATURE_TILE)] = functools.reduce(
+            jnp.add, [last_product(upper_half + b, column) for b in range(n_dp - 1)]
+        )
+        return 0
+
+    def last_tile(i, _):
+        column = pl.multiple_of(i * FEATURE_TILE, FEATURE_TILE)
+        total = partial[:, pl.ds(column, FEATURE_TILE)] + last_product(farthest, column)
+        out_ref[full * CHUNK : rows, pl.ds(column, FEATURE_TILE)] = total.astype(out_ref.dtype)
+        return 0
+
+    lax.fori_loop(0, features // FEATURE_TILE, partial_tile, 0)
     lax.fori_loop(0, full, finish_chunk, 0)
     arrive(chunks[-1][0], chunks[-1][1], full, 3)
-    multiply(full * CHUNK, rest)
+    lax.fori_loop(0, features // FEATURE_TILE, last_tile, 0)
 
     def sent(copy):
         copy.wait_send()
@@ -523,6 +548,7 @@
             pltpu.VMEM((rows, width), jnp.bfloat16),
             pltpu.VMEM((rows, width), jnp.bfloat16),
             pltpu.VMEM((rows, width), jnp.bfloat16),
+            pltpu.VMEM((rows % CHUNK, features), jnp.float32),
             pltpu.VMEM((n_seq, 2, heads, group * CAP, HEAD_WIDTH), jnp.bfloat16),
             pltpu.VMEM((heads, rows, query_rows), jnp.float32),
             pltpu.VMEM((heads, rows, query_rows), jnp.float32),

time: 140 us -> 138 us (0.986)
  Pallas kernels: 137 us -> 135 us
    pallas_call x1, Pallas kernels: 137 us -> 135 us  [body_kernel(): pl.pallas_call(functools.partial(kernel, sizes), out_shape=pltpu.VMEM((ro...]
where the time goes in v5:
time: 138 us
  Pallas kernels  135 us (98%)
  local copies, waits for them, and re-layouts  2.8 us (2%)
    pallas_call x1, Pallas kernels, body_kernel(): pl.pallas_call(functools.partial(kernel, sizes), out_shape=pltpu.VMEM((ro...  135 us
    unnamed x1, local copies, waits for them, and re-layouts  2.8 us

profile of v5, /device:TPU:0, one launch (start us, length us, event | category | flops | bytes accessed | tf_op | source)
XLA Modules:
  0.0 137.7 jit_solution(10603180687744253607)
XLA Ops:
  0.0 134.9 %shard_map.91 = bf16[1608,2048]{1,0:T(8,128)(2,1)S(1)} custom-call(s32[1,128]{1,0:T(1,128)} %bitcast.8, s32[2]{0:T(128)} %limit_ref.1, bf16[128,2048]{1,0:T(8,128)(2,1)} %query_hbm.1, bf16[128,2048]{1,0:T(8,128)(2,1)} %grad_hbm.1, bf16[1608,256]{1,0:T(8,128)(2,1)} %bitcast.6, bf16[1608,256]{1,0:T(8,128)(2,1)} %bitcast.7, f32[1,128]{1,0:T(1,128)} %bitcast.9, ...), custom_call_target="tpu_custom_call" | custom-call | tf_op jit(solution)/shard_map/pallas_call | solution.py:530
  134.9 2.8 %copy.11 = bf16[1,1608,2048]{2,1,0:T(8,128)(2,1)} copy(bf16[1,1608,2048]{2,1,0:T(8,128)(2,1)S(1)} %bitcast.5) | data formatting | bytes 13172736
